TPU v7x, 256 devices: a whole 4x4x8 slice. The times are simulated.
256 devices in a mesh: dp: 32 (over y, z_lo, core), seq: 8 (over z_hi, x).
Axes of the slice: x: 4, y: 4, z: 8 (z_hi: 2, z_lo: 4; z = z_hi * 4 + z_lo), core: 2. Of those that a mesh axis runs over, the one named last changes fastest.
Arguments:
- stream_in: bfloat16 [32, 1024, 768], P('dp', 'seq'), may hold values from -30 to 30
- queries: bfloat16 [32, 1024, 768], P('dp', 'seq'), may hold values from -5.6 to 5.6
- key_rows: bfloat16 [32, 1024, 768], P('dp', 'seq'), may hold values from -5.6 to 5.6
- value_rows: bfloat16 [32, 1024, 768], P('dp', 'seq'), may hold values from -6 to 6
- conv_weight: bfloat16 [768, 5, 768], P('dp'), may hold values from -0.09375 to 0.09375
- cotangent: bfloat16 [32, 1024, 768], P('dp', 'seq'), may hold values from -6 to 6
Outputs:
- grad_stream: bfloat16 [32, 1024, 768], P('dp', 'seq')
- grad_queries: bfloat16 [32, 1024, 768], P('dp', 'seq')
- grad_keys: bfloat16 [32, 1024, 768], P('dp', 'seq')
- grad_values: bfloat16 [32, 1024, 768], P('dp', 'seq')
- grad_weight: float32 [768, 5, 768], P('dp')
All inputs are finite; a program needn't handle non-finite values.
Results may differ from a plain program's by a relative error of at most 0.017.
Values may be sent and summed in bfloat16 or wider, within the bound.
A program may use at most 128 MiB of HBM per device.

v0:
```python
import jax
import jax.numpy as jnp
from jax import lax
from jax.sharding import PartitionSpec as P

HEADS = 8
HEAD_DIM = 96
TAPS = 5


def padded(block, sides, width):
    for axis, dim in sides:
        count = lax.axis_size(axis)
        forward = [(i, i + 1) for i in range(count - 1)]
        backward = [(target, source) for source, target in forward]
        low = lax.ppermute(
            lax.slice_in_dim(block, block.shape[dim] - width, None, axis=dim), axis, forward
        )
        high = lax.ppermute(lax.slice_in_dim(block, 0, width, axis=dim), axis, backward)
        block = jnp.concatenate([low, block, high], axis=dim)
    return block


def activate(stream):
    square = jnp.mean(stream * stream, axis=-1, keepdims=True)
    return jax.nn.gelu(stream * lax.rsqrt(square + 1e-06), approximate=True)


def attend_forward(query, keys, values, scale):
    scores = jnp.einsum("rhd,nhd->hrn", query, keys, preferred_element_type=jnp.float32) * scale
    top = jnp.max(scores, axis=-1, keepdims=True)
    expo = jnp.exp(scores - top)
    total = jnp.sum(expo, axis=-1, keepdims=True)
    expo_b = expo.astype(jnp.bfloat16)
    attended = jnp.einsum("hrn,nhd->rhd", expo_b, values, preferred_element_type=jnp.float32)
    attended = attended / jnp.transpose(total, (1, 0, 2))
    return (expo, total, attended)


def attend_back(keys, values, expo, total, attended, dout, scale):
    probs = expo / total
    probs_b = probs.astype(jnp.bfloat16)
    delta = jnp.transpose(jnp.sum(dout.astype(jnp.float32) * attended, axis=-1), (1, 0))[:, :, None]
    dprob = jnp.einsum("rhd,nhd->hrn", dout, values, preferred_element_type=jnp.float32)
    dscore = (probs * (dprob - delta)).astype(jnp.bfloat16)
    grad_query = (
        jnp.einsum("hrn,nhd->rhd", dscore, keys, preferred_element_type=jnp.float32) * scale
    )
    return (dscore, probs_b, grad_query)


def body(stream_in, queries, key_rows, value_rows, conv_weight, cotangent):
    rows = queries.shape[1]
    channels = queries.shape[2]
    dp_count = lax.axis_size("dp")
    seq_count = lax.axis_size("seq")
    length = rows * seq_count
    scale = HEAD_DIM ** (-0.5)
    half = TAPS // 2
    query_local = queries[0].reshape(rows, HEADS, HEAD_DIM)
    keys_all, values_all = (
        lax.all_gather(key_rows, "seq", axis=1, tiled=True),
        lax.all_gather(value_rows, "seq", axis=1, tiled=True),
    )
    keys_full = keys_all[0].reshape(length, HEADS, HEAD_DIM)
    values_full = values_all[0].reshape(length, HEADS, HEAD_DIM)
    expo, total, attended = attend_forward(query_local, keys_full, values_full, scale)
    attended_flat = attended.reshape(rows, channels)
    stream = (stream_in[0].astype(jnp.float32) + attended_flat).astype(jnp.bfloat16)
    hidden, pullback = jax.vjp(activate, stream.astype(jnp.float32))
    hidden_b = hidden.astype(jnp.bfloat16)
    full_weight = lax.all_gather(conv_weight, "dp", axis=0, tiled=True)
    extended = padded(jnp.stack([hidden_b, cotangent[0]]), (("seq", 1),), half)
    hid_ext = extended[0]
    cot_ext = extended[1]
    cot_local = cotangent[0]
    windows = jnp.stack([hid_ext[tap : tap + rows] for tap in range(TAPS)], axis=1).reshape(
        rows, TAPS * channels
    )
    norm_factor = 1.0 / jnp.sqrt(jnp.float32(dp_count * length))
    owned = lax.psum_scatter(
        jnp.einsum("to,tk->ok", cot_local, windows, preferred_element_type=jnp.float32),
        "dp",
        scatter_dimension=0,
        tiled=True,
    )
    summed = lax.psum(owned, "seq")
    grad_weight = (summed * norm_factor).reshape(summed.shape[0], TAPS, channels)
    back = jnp.zeros((rows, channels), jnp.float32)
    for tap in range(TAPS):
        start = 2 * half - tap
        back = back + jnp.dot(
            cot_ext[start : start + rows],
            full_weight[:, tap, :],
            preferred_element_type=jnp.float32,
        )
    grad_stream = (cot_local.astype(jnp.float32) + pullback(back)[0]).astype(jnp.bfloat16)
    dout = grad_stream.reshape(rows, HEADS, HEAD_DIM)
    dscore, probs_b, grad_query = attend_back(
        keys_full, values_full, expo, total, attended, dout, scale
    )
    key_part = (
        jnp.einsum("hrn,rhd->nhd", dscore, query_local, preferred_element_type=jnp.float32) * scale
    )
    value_part = jnp.einsum("hrn,rhd->nhd", probs_b, dout, preferred_element_type=jnp.float32)
    key_sum, value_sum = (
        lax.psum_scatter(
            key_part.reshape(1, length, channels).astype(jnp.bfloat16),
            "seq",
            scatter_dimension=1,
            tiled=True,
        ).astype(jnp.float32),
        lax.psum_scatter(
            value_part.reshape(1, length, channels).astype(jnp.bfloat16),
            "seq",
            scatter_dimension=1,
            tiled=True,
        ).astype(jnp.float32),
    )
    grad_queries = grad_query.reshape(1, rows, channels).astype(jnp.bfloat16)
    grad_keys = key_sum.astype(jnp.bfloat16)
    grad_values = value_sum.astype(jnp.bfloat16)
    return (grad_stream[None], grad_queries, grad_keys, grad_values, grad_weight)


def solution(mesh):
    in_specs = (
        P("dp", "seq", None),
        P("dp", "seq", None),
        P("dp", "seq", None),
        P("dp", "seq", None),
        P("dp", None, None),
        P("dp", "seq", None),
    )
    out_specs = (
        P("dp", "seq", None),
        P("dp", "seq", None),
        P("dp", "seq", None),
        P("dp", "seq", None),
        P("dp", None, None),
    )
    return jax.shard_map(body, mesh=mesh, in_specs=in_specs, out_specs=out_specs, check_vma=False)
```

profile of v0, /device:TPU:176, one launch (start us, length us, event | category | flops | bytes accessed | tf_op | source)
XLA Modules:
  0.0 701.4 jit_solution(6786424331102835818)
XLA Ops:
  11.7 64.1 %all-gather.4.cloned.1.call-done = bf16[1,1024,768]{2,1,0:T(8,128)(2,1)} async-done(((bf16[1,128,768]{2,1,0:T(8,128)(2,1)}), bf16[1,1024,768]{2,1,0:T(8,128)(2,1)}) %all-gather.4.cloned.1.call-update) | async-done | bytes 1572880 | tf_op jit(solution)/shard_map/all_gather | solution.py:62
  75.8 1.7 copy.36
  77.5 65.9 %all-gather.6.cloned.1.call-done = bf16[1,1024,768]{2,1,0:T(8,128)(2,1)} async-done(((bf16[1,128,768]{2,1,0:T(8,128)(2,1)}), bf16[1,1024,768]{2,1,0:T(8,128)(2,1)}) %all-gather.6.cloned.1.call-update) | async-done | bytes 1572880 | tf_op jit(solution)/shard_map/all_gather | solution.py:63
  143.4 2.6 copy.37
  147.7 1.7 copy-done.10
  150.8 3.1 collective-permute-start.1
  153.9 8.8 %collective-permute-start = (bf16[2,2,768]{2,1,0:T(2,128)(2,1)S(1)}, bf16[2,2,768]{2,1,0:T(2,128)(2,1)S(1)}, u32[]{:S(2)}, u32[]{:S(2)}) collective-permute-start(bf16[2,2,768]{2,1,0:T(2,128)(2,1)S(1)} %get-tuple-element.23), channel_id=1, source_target_pairs={{1,0},{2,1},{3,2},{4,3},{5,4},{6,5},{7,6},{9,8},{10,9},{11,10},{12... | collective-permute-start | bytes 18440 | tf_op jit(solution)/shard_map/ppermute | solution.py:19
  167.8 1.6 copy.44
  169.4 6.0 convolution_bitcast_fusion
  175.4 12.5 %copy.47 = f32[768,3840]{1,0:T(8,128)} copy(f32[768,3840]{0,1:T(8,128)} %convolution_bitcast_fusion) | data formatting | bytes 23592960
  188.2 21.4 %all-gather.8.cloned.1.call-done = bf16[768,5,768]{2,0,1:T(8,128)(2,1)} async-done(((bf16[24,5,768]{2,0,1:T(8,128)(2,1)}), bf16[768,5,768]{2,0,1:T(8,128)(2,1)}) %all-gather.8.cloned.1.call-update) | async-done | bytes 5898256 | tf_op jit(solution)/shard_map/all_gather | solution.py:72
  212.8 1.6 convolution_add_fusion.2
  216.0 1.9 fusion.41
  218.3 141.7 %reduce-scatter.10.cloned.1.call-done = f32[24,3840]{1,0:T(8,128)} async-done(((f32[768,3840]{1,0:T(8,128)}), f32[24,3840]{1,0:T(8,128)}) %reduce-scatter.10.cloned.1.call-update) | async-done | bytes 368656
  360.0 2.8 copy.48
  362.9 4.6 fusion.9
  367.5 2.7 copy.43
  371.5 3.9 multiply_convert_fusion
  377.3 1.7 copy.42
  379.0 2.4 fusion.16
  382.2 126.5 %all-reduce.2.cloned.1.call-done = f32[24,3840]{0,1:T(8,128)} async-done(((f32[24,3840]{0,1:T(8,128)}), f32[24,3840]{0,1:T(8,128)}) %all-reduce.2.cloned.1.call-update) | async-done | bytes 368656 | tf_op jit(solution)/shard_map/psum | solution.py:87
  508.7 1.7 broadcast_multiply_fusion
  511.7 92.0 %reduce-scatter.8.cloned.1.call-done = bf16[1,128,768]{2,1,0:T(8,128)(2,1)} async-done(((bf16[1,1024,768]{2,1,0:T(8,128)(2,1)}), bf16[1,128,768]{2,1,0:T(8,128)(2,1)}) %reduce-scatter.8.cloned.1.call-update) | async-done | bytes 196624 | tf_op jit(solution)/shard_map/reduce_scatter | solution.py:113
  603.7 90.9 %reduce-scatter.6.cloned.1.call-done = bf16[1,128,768]{2,1,0:T(8,128)(2,1)} async-done(((bf16[1,1024,768]{2,1,0:T(8,128)(2,1)}), bf16[1,128,768]{2,1,0:T(8,128)(2,1)}) %reduce-scatter.6.cloned.1.call-update) | async-done | bytes 196624 | tf_op jit(solution)/shard_map/reduce_scatter | solution.py:107
  (70 shorter events, 23.3 us)
Async XLA Ops:
  7.2 68.6 %all-gather.4.cloned.1.call-start = ((), (), s32[]{:S(2)}) async-start(), calls=%async_computation.3 | async-start | bytes 1769472 | tf_op jit(solution)/shard_map/all_gather | solution.py:62
  7.9 135.5 %all-gather.6.cloned.1.call-start = ((), (), s32[]{:S(2)}) async-start(), calls=%async_computation.4 | async-start | bytes 1769472 | tf_op jit(solution)/shard_map/all_gather | solution.py:63
  8.6 200.9 %all-gather.8.cloned.1.call-start = ((), (), s32[]{:S(2)}) async-start(), calls=%async_computation.5 | async-start | bytes 6082560 | tf_op jit(solution)/shard_map/all_gather | solution.py:72
  9.4 350.6 %reduce-scatter.10.cloned.1.call-start = ((), (), s32[]{:S(2)}) async-start(), calls=%async_computation.9 | async-start | bytes 12165120
  10.5 135.4 %copy-start.7 = (bf16[1,128,768]{1,2,0:T(8,128)(2,1)}, bf16[1,128,768]{1,2,0:T(8,128)(2,1)S(1)}, u32[]{:S(2)}) copy-start(bf16[1,128,768]{1,2,0:T(8,128)(2,1)S(1)} %copy.35) | copy-start | bytes 589828
  146.8 3.6 copy-start
  146.8 2.6 copy-start.10
  149.4 1.2 copy-start.9
  149.4 1.4 copy-start.2
  150.8 11.9 %collective-permute-start.1 = (bf16[2,2,768]{2,1,0:T(2,128)(2,1)S(1)}, bf16[2,2,768]{2,1,0:T(2,128)(2,1)S(1)}, u32[]{:S(2)}, u32[]{:S(2)}) collective-permute-start(bf16[2,2,768]{2,1,0:T(2,128)(2,1)S(1)} %get-tuple-element.22), channel_id=1, source_target_pairs={{0,1},{1,2},{2,3},{3,4},{4,5},{5,6},{6,7},{8,9},{9,10},{10,11},{11... | collective-permute-start | bytes 18440 | tf_op jit(solution)/shard_map/ppermute | solution.py:16
  153.9 10.1 %collective-permute-start = (bf16[2,2,768]{2,1,0:T(2,128)(2,1)S(1)}, bf16[2,2,768]{2,1,0:T(2,128)(2,1)S(1)}, u32[]{:S(2)}, u32[]{:S(2)}) collective-permute-start(bf16[2,2,768]{2,1,0:T(2,128)(2,1)S(1)} %get-tuple-element.23), channel_id=1, source_target_pairs={{1,0},{2,1},{3,2},{4,3},{5,4},{6,5},{7,6},{9,8},{10,9},{11,10},{12... | collective-permute-start | bytes 18440 | tf_op jit(solution)/shard_map/ppermute | solution.py:19
  164.1 2.9 copy-start.3
  164.1 2.9 copy-start.5
  187.9 21.7 %copy-start.6 = (bf16[2,130,768]{2,1,0:T(8,128)(2,1)S(1)}, bf16[2,130,768]{2,1,0:T(8,128)(2,1)}, u32[]{:S(2)}) copy-start(bf16[2,130,768]{2,1,0:T(8,128)(2,1)} %copy-done.5) | copy-start | bytes 1198084
  187.9 320.8 %all-reduce.2.cloned.1.call-start = ((), (), s32[]{:S(2)}) async-start(), calls=%async_computation.8 | async-start | bytes 3932160 | tf_op jit(solution)/shard_map/psum | solution.py:87
  188.2 26.2 %copy-start.4 = (bf16[2,130,768]{2,1,0:T(8,128)(2,1)S(1)}, bf16[2,130,768]{2,1,0:T(8,128)(2,1)}, u32[]{:S(2)}) copy-start(bf16[2,130,768]{2,1,0:T(8,128)(2,1)} %copy-done.3) | copy-start | bytes 1198084
  218.1 144.7 %copy-start.12 = (bf16[128,768]{1,0:T(8,128)(2,1)}, bf16[128,768]{1,0:T(8,128)(2,1)S(1)}, u32[]{:S(2)}) copy-start(bf16[128,768]{1,0:T(8,128)(2,1)S(1)} %fusion.43) | copy-start | bytes 589828
  218.3 144.6 %copy-start.13 = (bf16[128,768]{0,1:T(8,128)(2,1)}, bf16[128,768]{0,1:T(8,128)(2,1)S(1)}, u32[]{:S(2)}) copy-start(bf16[128,768]{0,1:T(8,128)(2,1)S(1)} %copy.41) | copy-start | bytes 589828
  362.8 240.9 %reduce-scatter.8.cloned.1.call-start = ((), (), s32[]{:S(2)}) async-start(), calls=%async_computation.7 | async-start | bytes 1769472 | tf_op jit(solution)/shard_map/reduce_scatter | solution.py:113
  367.5 3.9 copy-start.11
  370.2 324.4 %reduce-scatter.6.cloned.1.call-start = ((), (), s32[]{:S(2)}) async-start(), calls=%async_computation.6 | async-start | bytes 1769472 | tf_op jit(solution)/shard_map/reduce_scatter | solution.py:107
  371.4 5.3 copy-start.8
  375.4 1.3 copy-start.1
Sparse Core Ops, SparseCore 0:
  10.6 65.1 all-gather.3
  78.4 64.9 all-gather.5
  145.2 64.3 all-gather.7
  212.0 147.8 reduce-scatter.9
  362.9 145.7 all-reduce.1
  513.2 90.4 reduce-scatter.7
  608.3 86.2 reduce-scatter.5
where the time goes:
time: 709 us; the launch traced here: 701 us
  waiting for transfers between devices  606 us (85%)
  local copies, waits for them, and re-layouts  37 us (5%)
  matrix products  27.6 us (4%)
  between operations  14.4 us (2%)
  starting transfers between devices  12.3 us (2%)
    unnamed x8, waiting for transfers between devices  144 us
    psum x1, waiting for transfers between devices, body(): summed = lax.psum(owned, 'seq')  127 us
    reduce_scatter x1, waiting for transfers between devices, body(): lax.psum_scatter(value_part.reshape(1, length, channels).astype(jnp.bfloa...  92 us
    reduce_scatter x1, waiting for transfers between devices, body(): lax.psum_scatter(key_part.reshape(1, length, channels).astype(jnp.bfloat1...  90.9 us
    all_gather x1, waiting for transfers between devices, body(): lax.all_gather(value_rows, 'seq', axis=1, tiled=True)  65.9 us
    all_gather x1, waiting for transfers between devices, body(): lax.all_gather(key_rows, 'seq', axis=1, tiled=True)  64.1 us
    unnamed x37, local copies, waits for them, and re-layouts  24.4 us
    all_gather x1, waiting for transfers between devices, body(): full_weight = lax.all_gather(conv_weight, 'dp', axis=0, tiled=True)  21.4 us
  transfers between devices with their start and end apart: 9, of which 8 were waited for; matrix products, arithmetic and copies ran while one was open for 9% of the time, Pallas kernels for 0%

commit v1 on v0

v1 whole, which is shorter than its diff:
```python
import jax
import jax.numpy as jnp
from jax import lax
from jax.experimental import pallas as pl
from jax.experimental.pallas import tpu as pltpu
from jax.sharding import PartitionSpec as P

HEADS = 8
HD = 96
TAPS = 5
ROWS = 128
CH = 768
QC = 192
W5 = TAPS * QC
EXT = 640
MESH = pl.DeviceIdType.MESH
F32 = jnp.float32
BF = jnp.bfloat16
NT = (((1,), (1,)), ((), ()))
SCALE = HD ** (-0.5)
LOG2E = 1.4426950408889634
GC = 0.7978845608028654
GA = 0.044715


def dot(a, b):
    return jnp.dot(a, b, preferred_element_type=F32)


def dot_nt(a, b):
    return lax.dot_general(a, b, NT, preferred_element_type=F32)


def lanes(parts):
    return jnp.concatenate(parts, axis=1)


def tr(value):
    return value.astype(F32).T


def copy_to(src, dst, send, recv, dev):
    return pltpu.make_async_remote_copy(
        src_ref=src, dst_ref=dst, send_sem=send, recv_sem=recv, device_id=dev, device_id_type=MESH
    )


def kernel(
    x_ref, q_ref, k_ref, v_ref, w_ref, c_ref,
    gs_out, dq_out, dk_out, dv_out, gw_out,
    qkv_s, qkv_r, kn, vn, st, ex, itot, attf, att_s, att_r,
    cblk, hal, cfull, coth, wbuf, wt, bk_s, bk_r, h_s, h_r, hw,
    gs_s, gs_r, dqa, d_s, d_r, gp, yb, zs, zb, ms, mb, fs, ob, strm,
    qkv_ss, qkv_rs, att_ss, att_rs, gs_ss, gs_rs, d_ss, d_rs,
    c_ss, c_rs, hal_ss, hal_rs, co_ss, co_rs,
    wy_ss, wy_rs, wz_ss, wz_rs, wc_ss, wc_rs,
    bk_ss, bk_rs, h_ss, h_rs, y_ss, y_rs, z_ss, z_rs, m_ss, m_rs, f_ss, f_rs,
):
    me = lax.axis_index("seq")
    dd = lax.axis_index("dp")
    zh = lax.div(me, 4)
    x = lax.rem(me, 4)
    y = lax.div(dd, 8)
    zl = lax.rem(lax.div(dd, 2), 4)
    c = lax.rem(dd, 2)
    oc = 1 - c
    z = zh * 4 + zl
    odp = y * 8 + zl * 2 + oc

    def seq_dev(p):
        return {"seq": p, "dp": dd}

    def xc_dev(xx, cc):
        return {"seq": zh * 4 + xx, "dp": y * 8 + zl * 2 + cc}

    def y_dev(yy):
        return {"seq": me, "dp": yy * 8 + zl * 2 + c}

    def z_dev(step):
        zz = lax.rem(z + step + 8, 8)
        return {"seq": lax.div(zz, 4) * 4 + x, "dp": y * 8 + lax.rem(zz, 4) * 2 + c}

    def loop(lo, hi, fn):
        def step(i, carry):
            fn(i)
            return carry

        lax.fori_loop(lo, hi, step, 0)

    hal[...] = jnp.zeros_like(hal)
    barrier = pltpu.get_barrier_semaphore()

    def hello(dev):
        pl.semaphore_signal(barrier, inc=1, device_id=dev, device_id_type=MESH)

    loop(1, 8, lambda r: hello(seq_dev(lax.rem(me + r, 8))))
    loop(0, 4, lambda xx: hello(xc_dev(xx, oc)))
    loop(1, 4, lambda r: hello(y_dev(lax.rem(y + r, 4))))
    for step in (1, -1, 2, -2):
        hello(z_dev(step))

    qkv_s[0] = tr(k_ref[...]).astype(BF).reshape(8, HD, ROWS)
    qkv_s[1] = tr(q_ref[...]).astype(BF).reshape(8, HD, ROWS)
    qkv_s[2] = tr(v_ref[...]).astype(BF).reshape(8, HD, ROWS)
    cblk[x] = tr(c_ref[...]).astype(BF)
    wbuf[c, zl, y] = w_ref[...]
    pl.semaphore_wait(barrier, 18)

    def exch(src, dst, ssem, rsem, p):
        return copy_to(src.at[p], dst.at[me], ssem.at[p], rsem.at[me], seq_dev(p))

    def exch_recv(src, dst, ssem, rsem, p):
        return copy_to(src.at[p], dst.at[p], ssem.at[p], rsem.at[p], seq_dev(p))

    def start_all(src, dst, ssem, rsem):
        loop(1, 8, lambda r: exch(src, dst, ssem, rsem, lax.rem(me + r, 8)).start())

    def recv_all(src, dst, ssem, rsem):
        loop(1, 8, lambda r: exch_recv(src, dst, ssem, rsem, lax.rem(me + r, 8)).wait_recv())

    def sent_all(src, dst, ssem, rsem):
        loop(1, 8, lambda r: exch_recv(src, dst, ssem, rsem, lax.rem(me + r, 8)).wait_send())

    def qkv(t):
        return qkv_s.at[t], qkv_r.at[t], qkv_ss.at[t], qkv_rs.at[t]

    for t in range(3):
        start_all(*qkv(t))

    def wy(yy, slot):
        return copy_to(wbuf.at[c, zl, slot], wbuf.at[c, zl, slot], wy_ss.at[yy], wy_rs.at[slot], y_dev(yy))

    loop(1, 4, lambda r: wy(lax.rem(y + r, 4), y).start())

    def cx(xx, slot):
        return copy_to(cblk.at[slot], cblk.at[slot], c_ss.at[xx], c_rs.at[slot], xc_dev(xx, c))

    loop(1, 4, lambda r: cx(lax.rem(x + r, 4), x).start())

    def edge(p, lo):
        rows = pl.ds(lo, 16)

        return copy_to(c_ref.at[rows], hal.at[pl.ds(lo, 16)], hal_ss.at[lax.rem(p, 4)], hal_rs, seq_dev(p))

    first = jnp.logical_and(zh == 1, x == 0)
    last = jnp.logical_and(zh == 0, x == 3)

    @pl.when(first)
    def _():
        loop(0, 4, lambda p: edge(p, 0).start())

    @pl.when(last)
    def _():
        loop(4, 8, lambda p: edge(p, 112).start())

    for t in range(3):
        qkv_r[t, me] = qkv_s[t, me]
    recv_all(*qkv(0))
    for b in range(8):
        kn[128 * b : 128 * b + 128, :] = tr(qkv_r[0, b]).astype(BF)
    recv_all(*qkv(1))

    loop(1, 4, lambda r: wy(lax.rem(y + r, 4), lax.rem(y + r, 4)).wait_recv())
    far = 2 - 4 * c

    def wz(i, step, slot):
        return copy_to(wbuf.at[c, slot], wbuf.at[c, slot], wz_ss.at[i], wz_rs.at[i], z_dev(step))

    wz(0, 1, zl).start()
    wz(1, -1, zl).start()
    wz(2, far, zl).start()

    recv_all(*qkv(2))
    for b in range(8):
        vn[128 * b : 128 * b + 128, :] = tr(qkv_r[2, b]).astype(BF)

    def pair(ref, t, i):
        return lanes([ref[t, 2 * i], ref[t, 2 * i + 1]])

    def forward(ib):
        qb = lanes([qkv_r[1, 2 * ib], qkv_r[1, 2 * ib + 1]])
        top = None
        for jb in range(4):
            s = dot(kn[256 * jb : 256 * jb + 256, :], qb)
            st[256 * jb : 256 * jb + 256, :] = s
            m = jnp.max(s, axis=0, keepdims=True)
            top = m if top is None else jnp.maximum(top, m)
        tot = jnp.zeros((1, 256), F32)
        acc = jnp.zeros((HD, 256), F32)
        for jb in range(4):
            e = jnp.exp2((st[256 * jb : 256 * jb + 256, :] - top) * (SCALE * LOG2E))
            ex[ib, 256 * jb : 256 * jb + 256, :] = e
            tot = tot + jnp.sum(e, axis=0, keepdims=True)
            acc = acc + dot(pair(qkv_r, 2, jb), e.astype(BF))
        inv = 1.0 / tot
        itot[ib] = inv
        att = acc * inv
        attf[ib] = att
        ab = att.astype(BF)
        for half in range(2):
            p = 2 * ib + half
            att_s[p] = ab[:, 128 * half : 128 * half + 128]

            @pl.when(p != me)
            def _():
                exch(att_s, att_r, att_ss, att_rs, p).start()

            @pl.when(p == me)
            def _():
                att_r[me] = att_s[me]

    loop(0, 4, forward)

    def wz_recv(i, step):
        slot = lax.rem(zl + step + 4, 4)
        return copy_to(wbuf.at[c, slot], wbuf.at[c, slot], wz_ss.at[i], wz_rs.at[i], z_dev(step))

    wz_recv(0, -1).wait_recv()
    wz_recv(1, 1).wait_recv()
    wz_recv(2, -far).wait_recv()

    def wc(slot):
        return copy_to(wbuf.at[slot], wbuf.at[slot], wc_ss, wc_rs, xc_dev(x, oc))

    wc(c).start()

    loop(1, 4, lambda r: cx(lax.rem(x + r, 4), lax.rem(x + r, 4)).wait_recv())

    @pl.when(zh == 0)
    def _():
        edge(0, 0).wait_recv()

    @pl.when(zh == 1)
    def _():
        edge(0, 112).wait_recv()

    halt = tr(hal[...]).astype(BF)
    for cc in range(2):
        for yy in range(4):
            lo = 192 * yy + 96 * cc
            for b in range(4):
                cfull[cc, yy, :, 128 * b : 128 * b + 128] = cblk[b, lo : lo + 96, :]
            cfull[cc, yy, :, 512:640] = halt[lo : lo + 96, :]

    co = copy_to(cfull.at[oc], coth, co_ss, co_rs, xc_dev(x, oc))
    co.start()

    wc(oc).wait_recv()
    for n in range(8):
        width = min(128, W5 - 128 * n)
        rows = []
        for cc in range(2):
            for yy in range(4):
                for j in range(4):
                    rows.append(wbuf[j % 2, 2 * cc + j // 2, yy, :, 128 * n : 128 * n + width].astype(F32))
        wt[128 * n : 128 * n + width, :] = jnp.concatenate(rows, axis=0).T.astype(BF)

    cot_all = cfull[...].reshape(CH, EXT)
    back_q = None
    for a in range(TAPS):
        part = dot(wt[QC * a : QC * a + QC, :], cot_all)
        shift = (a - 2) % EXT
        if shift:
            part = pltpu.roll(part, shift, 1)
        back_q = part if back_q is None else back_q + part
    back_b = back_q.astype(BF)
    for b in range(4):
        bk_s[b] = back_b[:, 128 * b : 128 * b + 128]
    bk_r[x] = bk_s[x]

    def bk(xx, slot_from, slot_to):
        return copy_to(bk_s.at[slot_from], bk_r.at[slot_to], bk_ss.at[xx], bk_rs.at[slot_to], xc_dev(xx, c))

    def bk_start(r):
        xx = lax.rem(x + r, 4)
        bk(xx, xx, x).start()

    def bk_wait(r):
        xx = lax.rem(x + r, 4)
        bk(xx, xx, xx).wait_recv()

    loop(1, 4, bk_start)

    xt = tr(x_ref[...])
    recv_all(att_s, att_r, att_ss, att_rs)
    u = (xt + att_r[...].astype(F32).reshape(CH, ROWS)).astype(BF).astype(F32)
    rs = lax.rsqrt(jnp.mean(u * u, axis=0, keepdims=True) + 1e-6)
    nn = u * rs
    th = jnp.tanh(GC * (nn + GA * (nn * nn * nn)))
    hid = (0.5 * nn * (1.0 + th)).astype(BF)
    h_s[...] = hid.reshape(4, QC, ROWS)
    h_r[c, x] = h_s[x]

    def hx(xx, cc):
        return copy_to(h_s.at[xx], h_r.at[c, x], h_ss.at[cc, xx], h_rs.at[c, x], xc_dev(xx, cc))

    def hx_recv(xx, cc):
        return copy_to(h_s.at[xx], h_r.at[cc, xx], h_ss.at[cc, xx], h_rs.at[cc, xx], xc_dev(xx, cc))

    loop(0, 4, lambda xx: hx(xx, oc).start())
    loop(1, 4, lambda r: hx(lax.rem(x + r, 4), c).start())

    loop(1, 4, bk_wait)
    bk_all = bk_r[...].astype(F32).reshape(CH, ROWS)
    slope = 0.5 * (1.0 + th) + 0.5 * nn * (1.0 - th * th) * (GC * (1.0 + 3.0 * GA * (nn * nn)))
    dn = bk_all * slope
    mean_dn = jnp.sum(dn * nn, axis=0, keepdims=True) * (1.0 / CH)
    du = rs * (dn - nn * mean_dn)
    gst = (cblk[x].astype(F32) + du).astype(BF)
    gs_s[...] = gst.reshape(8, HD, ROWS)
    gs_r[me] = gs_s[me]
    start_all(gs_s, gs_r, gs_ss, gs_rs)
    gs_out[...] = tr(gst).astype(BF)

    loop(0, 4, lambda xx: hx_recv(xx, oc).wait_recv())
    loop(1, 4, lambda r: hx_recv(lax.rem(x + r, 4), c).wait_recv())
    for cc in range(2):
        hv = lanes([h_r[cc, b] for b in range(4)] + [jnp.zeros((QC, 128), BF)]).astype(F32)
        for a in range(TAPS):
            shift = (2 - a) % EXT
            hw[cc, QC * a : QC * a + QC, :] = (pltpu.roll(hv, shift, 1) if shift else hv).astype(BF)
    co.wait_recv()
    own_c = cfull[c].reshape(384, EXT)
    oth_c = coth[...].reshape(384, EXT)
    for lo, hi in ((0, 512), (512, W5)):
        part = dot_nt(own_c, hw[c, lo:hi, :]) + dot_nt(oth_c, hw[oc, lo:hi, :])
        gp[:, :, lo:hi] = part.astype(BF).reshape(4, 96, hi - lo)

    def ys(r):
        yy = lax.rem(y + r, 4)
        return copy_to(gp.at[yy], yb.at[y], y_ss.at[yy], y_rs.at[y], y_dev(yy))

    def ys_recv(r):
        yy = lax.rem(y + r, 4)
        return copy_to(gp.at[yy], yb.at[yy], y_ss.at[yy], y_rs.at[yy], y_dev(yy))

    loop(1, 4, lambda r: ys(r).start())

    recv_all(gs_s, gs_r, gs_ss, gs_rs)
    dqa[...] = jnp.zeros_like(dqa)
    deltas = []
    for ib in range(4):
        gsb = lanes([gs_r[2 * ib], gs_r[2 * ib + 1]]).astype(F32)
        deltas.append(jnp.sum(gsb * attf[ib], axis=0, keepdims=True))
    delta = lanes(deltas)
    st[0:1, :] = deltas[0]
    for ib in range(4):
        st[ib : ib + 1, :] = deltas[ib]

    def ds_ex(t, p):
        return copy_to(d_s.at[t, p], d_r.at[t, me], d_ss.at[t, p], d_rs.at[t, me], seq_dev(p))

    def out_block(t, p):
        @pl.when(p != me)
        def _():
            ds_ex(t, p).start()

        @pl.when(p == me)
        def _():
            d_r[t, me] = d_s[t, me]

    def backward(jb):
        rows = pl.ds(pl.multiple_of(256 * jb, 256), 256)
        vb = vn[rows, :]
        kb = lanes([qkv_r[0, 2 * jb], qkv_r[0, 2 * jb + 1]])
        dk = jnp.zeros((HD, 256), F32)
        dv = jnp.zeros((HD, 256), F32)
        for ib in range(4):
            gsb = lanes([gs_r[2 * ib], gs_r[2 * ib + 1]])
            dp = dot(vb, gsb)
            p = ex[ib, rows, :] * itot[ib]
            ds = (p * (dp - st[ib : ib + 1, :])).astype(BF)
            dv = dv + dot_nt(gsb, p.astype(BF))
            dk = dk + dot_nt(pair(qkv_r, 1, ib), ds)
            dqa[:, 256 * ib : 256 * ib + 256] += dot(kb, ds)
        dkb = (dk * SCALE).astype(BF)
        dvb = dv.astype(BF)
        for half in range(2):
            p = 2 * jb + half
            d_s[0, p] = dkb[:, 128 * half : 128 * half + 128]
            d_s[1, p] = dvb[:, 128 * half : 128 * half + 128]
            out_block(0, p)
            out_block(1, p)

    loop(0, 2, backward)

    loop(1, 4, lambda r: ys_recv(r).wait_recv())
    acc = gp[y].astype(F32)
    for r in range(1, 4):
        acc = acc + yb[lax.rem(y + r, 4)].astype(F32)
    zs[...] = acc.astype(BF).reshape(2, 48, W5)
    owner = lax.div(zl, 2) == c

    def zsend(kk):
        r = lax.rem(zl - (2 * c + kk) + 4, 4)
        step = 4 * lax.div(r, 3) - r
        return r, copy_to(zs.at[kk], zb.at[r], z_ss.at[kk], z_rs.at[r], z_dev(step))

    for kk in range(2):
        r, cp = zsend(kk)

        @pl.when(r != 0)
        def _():
            cp.start()

    loop(2, 4, backward)

    dq_all = (dqa[...] * SCALE).astype(BF)
    for p in range(8):
        d_s[2, p] = dq_all[:, 128 * p : 128 * p + 128]
        out_block(2, p)

    def mx():
        return copy_to(ms, mb, m_ss, m_rs, seq_dev(lax.rem(me + 4, 8)))

    def fx(xx, cc):
        return copy_to(fs.at[cc], ob.at[x], f_ss.at[cc, xx], f_rs.at[x], xc_dev(xx, cc))

    def fx_recv(xx):
        return copy_to(fs.at[c], ob.at[xx], f_ss.at[c, xx], f_rs.at[xx], xc_dev(xx, c))

    @pl.when(owner)
    def _():
        for r, step in ((1, 1), (2, 2), (3, -1)):
            copy_to(zs.at[0], zb.at[r], z_ss.at[0], z_rs.at[r], z_dev(step)).wait_recv()
        tot = zs[lax.rem(zl, 2)].astype(F32)
        for r in range(1, 4):
            tot = tot + zb[r].astype(F32)
        ms[...] = tot
        mx().start()
        mx().wait_recv()
        norm = 1.0 / jnp.sqrt(F32(32 * 1024))
        both = (ms[...] + mb[...]) * norm
        fs[...] = both.reshape(2, 24, W5)
        loop(0, 4, lambda xx: fx(xx, oc).start())
        loop(1, 4, lambda r: fx(lax.rem(x + r, 4), c).start())
        ob[x] = fs[c]

    def d_all(t):
        return d_s.at[t], d_r.at[t], d_ss.at[t], d_rs.at[t]

    for t, out in ((0, dk_out), (1, dv_out), (2, dq_out)):
        recv_all(*d_all(t))
        out[...] = tr(d_r[t].reshape(CH, ROWS)).astype(BF)

    loop(1, 4, lambda r: fx_recv(lax.rem(x + r, 4)).wait_recv())

    @pl.when(jnp.logical_not(owner))
    def _():
        fx_recv(x).wait_recv()

    for a in range(TAPS):
        gw_out[:, a, :] = lanes([ob[b, :, QC * a : QC * a + QC] for b in range(4)])

    for t in range(3):
        sent_all(*qkv(t))
        sent_all(*d_all(t))
    sent_all(att_s, att_r, att_ss, att_rs)
    sent_all(gs_s, gs_r, gs_ss, gs_rs)
    loop(1, 4, lambda r: wy(lax.rem(y + r, 4), y).wait_send())
    loop(1, 4, lambda r: cx(lax.rem(x + r, 4), x).wait_send())

    @pl.when(first)
    def _():
        loop(0, 4, lambda p: edge(p, 0).wait_send())

    @pl.when(last)
    def _():
        loop(4, 8, lambda p: edge(p, 112).wait_send())

    wz(0, 1, zl).wait_send()
    wz(1, -1, zl).wait_send()
    wz(2, far, zl).wait_send()
    wc(c).wait_send()
    co.wait_send()
    loop(1, 4, lambda r: bk(lax.rem(x + r, 4), lax.rem(x + r, 4), x).wait_send())
    loop(0, 4, lambda xx: hx(xx, oc).wait_send())
    loop(1, 4, lambda r: hx(lax.rem(x + r, 4), c).wait_send())
    loop(1, 4, lambda r: ys(r).wait_send())
    for kk in range(2):
        r, cp = zsend(kk)

        @pl.when(r != 0)
        def _():
            cp.wait_send()

    @pl.when(owner)
    def _():
        mx().wait_send()
        loop(0, 4, lambda xx: fx(xx, oc).wait_send())
        loop(1, 4, lambda r: fx(lax.rem(x + r, 4), c).wait_send())


def body(stream_in, queries, key_rows, value_rows, conv_weight, cotangent):
    x = lax.rem(lax.axis_index("seq"), 4)
    w = lax.dynamic_slice(conv_weight, (0, 0, x * QC), (24, TAPS, QC)).reshape(24, W5)
    nat = jax.ShapeDtypeStruct((ROWS, CH), BF)
    V = pltpu.VMEM
    blk = (8, HD, ROWS)
    scratch = [
        V((3,) + blk, BF), V((3,) + blk, BF),
        V((1024, HD), BF), V((1024, HD), BF),
        V((1024, 256), F32), V((4, 1024, 256), F32), V((4, 1, 256), F32), V((4, HD, 256), F32),
        V(blk, BF), V(blk, BF),
        V((4, CH, ROWS), BF), V((ROWS, CH), BF), V((2, 4, 96, EXT), BF), V((4, 96, EXT), BF),
        V((2, 4, 4, 24, W5), BF), V((W5, CH), BF),
        V((4, QC, ROWS), BF), V((4, QC, ROWS), BF),
        V((4, QC, ROWS), BF), V((2, 4, QC, ROWS), BF), V((2, W5, EXT), BF),
        V(blk, BF), V(blk, BF), V((HD, 1024), F32), V((3,) + blk, BF), V((3,) + blk, BF),
        V((4, 96, W5), BF), V((4, 96, W5), BF), V((2, 48, W5), BF), V((4, 48, W5), BF),
        V((48, W5), F32), V((48, W5), F32), V((2, 24, W5), F32), V((4, 24, W5), F32),
        V((8, 128), F32),
    ]
    D = pltpu.SemaphoreType.DMA
    sems = [
        D((3, 8)), D((3, 8)), D((8,)), D((8,)), D((8,)), D((8,)), D((3, 8)), D((3, 8)),
        D((4,)), D((4,)), D((4,)), D, D, D,
        D((4,)), D((4,)), D((3,)), D((3,)), D, D,
        D((4,)), D((4,)), D((2, 4)), D((2, 4)), D((4,)), D((4,)), D((2,)), D((4,)), D, D,
        D((2, 4)), D((4,)),
    ]
    vm = pl.BlockSpec(memory_space=pltpu.VMEM)
    gs, dq, dk, dv, gw = pl.pallas_call(
        kernel,
        out_shape=(nat, nat, nat, nat, jax.ShapeDtypeStruct((24, TAPS, CH), F32)),
        in_specs=[vm] * 6,
        out_specs=(vm,) * 5,
        scratch_shapes=scratch + sems,
        compiler_params=pltpu.CompilerParams(
            collective_id=0, has_side_effects=True, vmem_limit_bytes=48 * 1024 * 1024
        ),
    )(stream_in[0], queries[0], key_rows[0], value_rows[0], w, cotangent[0])
    return gs[None], dq[None], dk[None], dv[None], gw


def solution(mesh):
    act = P("dp", "seq", None)
    wsp = P("dp", None, None)
    return jax.shard_map(
        body,
        mesh=mesh,
        in_specs=(act, act, act, act, wsp, act),
        out_specs=(act, act, act, act, wsp),
        check_vma=False,
    )
```

time: 709 us -> 110 us (0.16)
  the two profiles are of different devices: /device:TPU:176 before, /device:TPU:8 now
where the time goes in v1:
time: 110 us
  Pallas kernels  101 us (92%)
  local copies, waits for them, and re-layouts  8.25 us (8%)
    pallas_call x1, Pallas kernels, body(): pl.pallas_call(kernel, out_shape=(nat, nat, nat, nat, jax.ShapeDtypeStruc...  101 us
    unnamed x17, local copies, waits for them, and re-layouts  8.04 us

profile of v1, /device:TPU:8, one launch (start us, length us, event | category | flops | bytes accessed | tf_op | source)
XLA Modules:
  0.0 109.6 jit_solution(13747796950962049904)
XLA Ops:
  0.6 0.0 copy-start
  0.7 0.9 copy-done
  1.6 0.0 copy-start.1
  1.6 0.0 copy-start.2
  1.6 0.1 constant_dynamic-slice_fusion
  1.7 0.1 reshape.13.w_ref
  1.8 0.7 copy-done.1
  2.5 0.1 copy-done.2
  2.6 0.0 copy-start.3
  2.6 0.9 copy-done.3
  3.5 0.0 copy-start.4
  3.5 0.9 copy-done.4
  4.4 0.0 copy-start.5
  4.4 0.9 copy-done.5
  5.4 100.7 %shard_map.101 = (bf16[128,768]{1,0:T(8,128)(2,1)S(1)}, bf16[128,768]{1,0:T(8,128)(2,1)S(1)}, bf16[128,768]{1,0:T(8,128)(2,1)S(1)}, bf16[128,768]{1,0:T(8,128)(2,1)S(1)}, f32[24,5,768]{2,1,0:T(8,128)S(1)}) custom-call(bf16[128,768]{1,0:T(8,128)(2,1)S(1)} %bitcast.13, bf16[128,768]{1,0:T(8,128)(2,1)S(1)} %bitcast.14, bf16[128,768]{1,0:T(8,128)(2,1)S(1)} %bitcast.15, ...), custom_call_target="tpu_custom_call" | custom-call | tf_op jit(solution)/shard_map/pallas_call | solution.py:523
  106.0 0.9 copy.14
  106.9 0.7 copy.19
  107.6 0.7 copy.20
  108.2 0.7 copy.21
  108.9 0.7 copy.22
  (1 shorter events, 0.0 us)
Async XLA Ops:
  0.6 0.9 copy-start
  1.6 0.9 copy-start.1
  1.6 1.0 copy-start.2
  2.6 0.9 copy-start.3
  3.5 0.9 copy-start.4
  4.4 0.9 copy-start.5

commit v2 on v1

--- a/solution.py
+++ b/solution.py
@@ -46,12 +46,14 @@
 
 
 def kernel(
-    x_ref, q_ref, k_ref, v_ref, w_ref, c_ref,
+    x_in, q_in, k_in, v_in, w_in, c_in,
+    gs_hbm, dq_hbm, dk_hbm, dv_hbm, gw_hbm,
     gs_out, dq_out, dk_out, dv_out, gw_out,
+    x_ref, q_ref, k_ref, v_ref, c_ref, w_ref,
     qkv_s, qkv_r, kn, vn, st, ex, itot, attf, att_s, att_r,
     cblk, hal, cfull, coth, wbuf, wt, bk_s, bk_r, h_s, h_r, hw,
-    gs_s, gs_r, dqa, d_s, d_r, gp, yb, zs, zb, ms, mb, fs, ob, strm,
-    qkv_ss, qkv_rs, att_ss, att_rs, gs_ss, gs_rs, d_ss, d_rs,
+    gs_s, gs_r, dqa, d_s, d_r, gp, yb, zs, zb, ms, mb, fs, ob,
+    in_sem, out_sem, qkv_ss, qkv_rs, att_ss, att_rs, gs_ss, gs_rs, d_ss, d_rs,
     c_ss, c_rs, hal_ss, hal_rs, co_ss, co_rs,
     wy_ss, wy_rs, wz_ss, wz_rs, wc_ss, wc_rs,
     bk_ss, bk_rs, h_ss, h_rs, y_ss, y_rs, z_ss, z_rs, m_ss, m_rs, f_ss, f_rs,
@@ -87,6 +89,23 @@
 
         lax.fori_loop(lo, hi, step, 0)
 
+    todo = {}
+
+    def owe(name, fn):
+        todo[name] = fn
+
+    def paid(name):
+        todo.pop(name)()
+
+    def finish():
+        for fn in list(todo.values()):
+            fn()
+
+    def store(i, src, dst):
+        save = pltpu.make_async_copy(src, dst, out_sem.at[i])
+        save.start()
+        owe(f"out{i}", save.wait)
+
     hal[...] = jnp.zeros_like(hal)
     barrier = pltpu.get_barrier_semaphore()
 
@@ -99,11 +118,22 @@
     for step in (1, -1, 2, -2):
         hello(z_dev(step))
 
-    qkv_s[0] = tr(k_ref[...]).astype(BF).reshape(8, HD, ROWS)
-    qkv_s[1] = tr(q_ref[...]).astype(BF).reshape(8, HD, ROWS)
-    qkv_s[2] = tr(v_ref[...]).astype(BF).reshape(8, HD, ROWS)
-    cblk[x] = tr(c_ref[...]).astype(BF)
-    wbuf[c, zl, y] = w_ref[...]
+    loads = []
+    for i, (src, dst) in enumerate(((k_in, k_ref), (q_in, q_ref), (v_in, v_ref), (c_in, c_ref), (x_in, x_ref), (w_in, w_ref))):
+        load = pltpu.make_async_copy(src, dst, in_sem.at[i])
+        load.start()
+        loads.append(load)
+    owe("x_in", loads[4].wait)
+    for i, ref in enumerate((k_ref, q_ref, v_ref)):
+        loads[i].wait()
+        qkv_s[i] = tr(ref[...]).astype(BF).reshape(8, HD, ROWS)
+    loads[5].wait()
+    for xs in range(4):
+
+        @pl.when(x == xs)
+        def _():
+            wbuf[c, y, zl] = lanes([w_ref[a, :, QC * xs : QC * xs + QC] for a in range(TAPS)])
+
     pl.semaphore_wait(barrier, 18)
 
     def exch(src, dst, ssem, rsem, p):
@@ -124,18 +154,44 @@
     def qkv(t):
         return qkv_s.at[t], qkv_r.at[t], qkv_ss.at[t], qkv_rs.at[t]
 
+    far = 2 - 4 * c
+
+    def wz(i, step, slot):
+        return copy_to(wbuf.at[c, y, slot], wbuf.at[c, y, slot], wz_ss.at[i], wz_rs.at[i], z_dev(step))
+
+    def wz_recv(i, step):
+        wz(i, step, lax.rem(zl + step + 4, 4)).wait_recv()
+
+    def wz_recv_all():
+        wz_recv(0, -1)
+        wz_recv(1, 1)
+        wz_recv(2, -far)
+
+    def wz_sent_all():
+        wz(0, 1, zl).wait_send()
+        wz(1, -1, zl).wait_send()
+        wz(2, far, zl).wait_send()
+
+    wz(0, 1, zl).start()
+    wz(1, -1, zl).start()
+    wz(2, far, zl).start()
+    owe("wz_r", wz_recv_all)
+    owe("wz_s", wz_sent_all)
     for t in range(3):
         start_all(*qkv(t))
-
-    def wy(yy, slot):
-        return copy_to(wbuf.at[c, zl, slot], wbuf.at[c, zl, slot], wy_ss.at[yy], wy_rs.at[slot], y_dev(yy))
-
-    loop(1, 4, lambda r: wy(lax.rem(y + r, 4), y).start())
-
+        owe(f"qkv_r{t}", lambda t=t: recv_all(*qkv(t)))
+        owe(f"qkv_s{t}", lambda t=t: sent_all(*qkv(t)))
+
+    loads[3].wait()
+    cblk[x] = tr(c_ref[...]).astype(BF)
+    for t in range(3):
+        qkv_r[t, me] = qkv_s[t, me]
     def cx(xx, slot):
         return copy_to(cblk.at[slot], cblk.at[slot], c_ss.at[xx], c_rs.at[slot], xc_dev(xx, c))
 
     loop(1, 4, lambda r: cx(lax.rem(x + r, 4), x).start())
+    owe("cx_r", lambda: loop(1, 4, lambda r: cx(lax.rem(x + r, 4), lax.rem(x + r, 4)).wait_recv()))
+    owe("cx_s", lambda: loop(1, 4, lambda r: cx(lax.rem(x + r, 4), x).wait_send()))
 
     def edge(p, lo):
         rows = pl.ds(lo, 16)
@@ -153,24 +209,41 @@
     def _():
         loop(4, 8, lambda p: edge(p, 112).start())
 
-    for t in range(3):
-        qkv_r[t, me] = qkv_s[t, me]
-    recv_all(*qkv(0))
+    def edge_recv():
+        @pl.when(zh == 0)
+        def _():
+            edge(0, 0).wait_recv()
+
+        @pl.when(zh == 1)
+        def _():
+            edge(0, 112).wait_recv()
+
+    def edge_sent():
+        @pl.when(first)
+        def _():
+            loop(0, 4, lambda p: edge(p, 0).wait_send())
+
+        @pl.when(last)
+        def _():
+            loop(4, 8, lambda p: edge(p, 112).wait_send())
+
+    owe("edge_r", edge_recv)
+    owe("edge_s", edge_sent)
+    paid("wz_r")
+
+    def wy(yy, slot):
+        return copy_to(wbuf.at[c, slot], wbuf.at[c, slot], wy_ss.at[yy], wy_rs.at[slot], y_dev(yy))
+
+    loop(1, 4, lambda r: wy(lax.rem(y + r, 4), y).start())
+    owe("wy_r", lambda: loop(1, 4, lambda r: wy(lax.rem(y + r, 4), lax.rem(y + r, 4)).wait_recv()))
+    owe("wy_s", lambda: loop(1, 4, lambda r: wy(lax.rem(y + r, 4), y).wait_send()))
+
+    paid("qkv_r0")
     for b in range(8):
         kn[128 * b : 128 * b + 128, :] = tr(qkv_r[0, b]).astype(BF)
-    recv_all(*qkv(1))
-
-    loop(1, 4, lambda r: wy(lax.rem(y + r, 4), lax.rem(y + r, 4)).wait_recv())
-    far = 2 - 4 * c
-
-    def wz(i, step, slot):
-        return copy_to(wbuf.at[c, slot], wbuf.at[c, slot], wz_ss.at[i], wz_rs.at[i], z_dev(step))
-
-    wz(0, 1, zl).start()
-    wz(1, -1, zl).start()
-    wz(2, far, zl).start()
-
-    recv_all(*qkv(2))
+    paid("qkv_r1")
+
+    paid("qkv_r2")
     for b in range(8):
         vn[128 * b : 128 * b + 128, :] = tr(qkv_r[2, b]).astype(BF)
 
@@ -210,30 +283,20 @@
                 att_r[me] = att_s[me]
 
     loop(0, 4, forward)
-
-    def wz_recv(i, step):
-        slot = lax.rem(zl + step + 4, 4)
-        return copy_to(wbuf.at[c, slot], wbuf.at[c, slot], wz_ss.at[i], wz_rs.at[i], z_dev(step))
-
-    wz_recv(0, -1).wait_recv()
-    wz_recv(1, 1).wait_recv()
-    wz_recv(2, -far).wait_recv()
+    owe("att_r", lambda: recv_all(att_s, att_r, att_ss, att_rs))
+    owe("att_s", lambda: sent_all(att_s, att_r, att_ss, att_rs))
+
+    paid("wy_r")
 
     def wc(slot):
         return copy_to(wbuf.at[slot], wbuf.at[slot], wc_ss, wc_rs, xc_dev(x, oc))
 
     wc(c).start()
-
-    loop(1, 4, lambda r: cx(lax.rem(x + r, 4), lax.rem(x + r, 4)).wait_recv())
-
-    @pl.when(zh == 0)
-    def _():
-        edge(0, 0).wait_recv()
-
-    @pl.when(zh == 1)
-    def _():
-        edge(0, 112).wait_recv()
-
+    owe("wc_r", lambda: wc(oc).wait_recv())
+    owe("wc_s", lambda: wc(c).wait_send())
+
+    paid("cx_r")
+    paid("edge_r")
     halt = tr(hal[...]).astype(BF)
     for cc in range(2):
         for yy in range(4):
@@ -244,15 +307,17 @@
 
     co = copy_to(cfull.at[oc], coth, co_ss, co_rs, xc_dev(x, oc))
     co.start()
-
-    wc(oc).wait_recv()
+    owe("co_r", co.wait_recv)
+    owe("co_s", co.wait_send)
+
+    paid("wc_r")
     for n in range(8):
         width = min(128, W5 - 128 * n)
         rows = []
         for cc in range(2):
             for yy in range(4):
                 for j in range(4):
-                    rows.append(wbuf[j % 2, 2 * cc + j // 2, yy, :, 128 * n : 128 * n + width].astype(F32))
+                    rows.append(wbuf[j % 2, yy, 2 * cc + j // 2, :, 128 * n : 128 * n + width].astype(F32))
         wt[128 * n : 128 * n + width, :] = jnp.concatenate(rows, axis=0).T.astype(BF)
 
     cot_all = cfull[...].reshape(CH, EXT)
@@ -280,9 +345,12 @@
         bk(xx, xx, xx).wait_recv()
 
     loop(1, 4, bk_start)
-
+    owe("bk_r", lambda: loop(1, 4, bk_wait))
+    owe("bk_s", lambda: loop(1, 4, lambda r: bk(lax.rem(x + r, 4), lax.rem(x + r, 4), x).wait_send()))
+
+    paid("x_in")
     xt = tr(x_ref[...])
-    recv_all(att_s, att_r, att_ss, att_rs)
+    paid("att_r")
     u = (xt + att_r[...].astype(F32).reshape(CH, ROWS)).astype(BF).astype(F32)
     rs = lax.rsqrt(jnp.mean(u * u, axis=0, keepdims=True) + 1e-6)
     nn = u * rs
@@ -300,7 +368,18 @@
     loop(0, 4, lambda xx: hx(xx, oc).start())
     loop(1, 4, lambda r: hx(lax.rem(x + r, 4), c).start())
 
-    loop(1, 4, bk_wait)
+    def hx_recv_all():
+        loop(0, 4, lambda xx: hx_recv(xx, oc).wait_recv())
+        loop(1, 4, lambda r: hx_recv(lax.rem(x + r, 4), c).wait_recv())
+
+    def hx_sent_all():
+        loop(0, 4, lambda xx: hx(xx, oc).wait_send())
+        loop(1, 4, lambda r: hx(lax.rem(x + r, 4), c).wait_send())
+
+    owe("hx_r", hx_recv_all)
+    owe("hx_s", hx_sent_all)
+
+    paid("bk_r")
     bk_all = bk_r[...].astype(F32).reshape(CH, ROWS)
     slope = 0.5 * (1.0 + th) + 0.5 * nn * (1.0 - th * th) * (GC * (1.0 + 3.0 * GA * (nn * nn)))
     dn = bk_all * slope
@@ -310,16 +389,19 @@
     gs_s[...] = gst.reshape(8, HD, ROWS)
     gs_r[me] = gs_s[me]
     start_all(gs_s, gs_r, gs_ss, gs_rs)
+    owe("gs_r", lambda: recv_all(gs_s, gs_r, gs_ss, gs_rs))
+    owe("gs_s", lambda: sent_all(gs_s, gs_r, gs_ss, gs_rs))
+
     gs_out[...] = tr(gst).astype(BF)
-
-    loop(0, 4, lambda xx: hx_recv(xx, oc).wait_recv())
-    loop(1, 4, lambda r: hx_recv(lax.rem(x + r, 4), c).wait_recv())
+    store(0, gs_out, gs_hbm)
+
+    paid("hx_r")
     for cc in range(2):
         hv = lanes([h_r[cc, b] for b in range(4)] + [jnp.zeros((QC, 128), BF)]).astype(F32)
         for a in range(TAPS):
             shift = (2 - a) % EXT
             hw[cc, QC * a : QC * a + QC, :] = (pltpu.roll(hv, shift, 1) if shift else hv).astype(BF)
-    co.wait_recv()
+    paid("co_r")
     own_c = cfull[c].reshape(384, EXT)
     oth_c = coth[...].reshape(384, EXT)
     for lo, hi in ((0, 512), (512, W5)):
@@ -335,8 +417,10 @@
         return copy_to(gp.at[yy], yb.at[yy], y_ss.at[yy], y_rs.at[yy], y_dev(yy))
 
     loop(1, 4, lambda r: ys(r).start())
-
-    recv_all(gs_s, gs_r, gs_ss, gs_rs)
+    owe("ys_r", lambda: loop(1, 4, lambda r: ys_recv(r).wait_recv()))
+    owe("ys_s", lambda: loop(1, 4, lambda r: ys(r).wait_send()))
+
+    paid("gs_r")
     dqa[...] = jnp.zeros_like(dqa)
     deltas = []
     for ib in range(4):
@@ -382,9 +466,20 @@
             out_block(0, p)
             out_block(1, p)
 
-    loop(0, 2, backward)
-
-    loop(1, 4, lambda r: ys_recv(r).wait_recv())
+    loop(0, 4, backward)
+    dq_all = (dqa[...] * SCALE).astype(BF)
+    for p in range(8):
+        d_s[2, p] = dq_all[:, 128 * p : 128 * p + 128]
+        out_block(2, p)
+
+    def d_all(t):
+        return d_s.at[t], d_r.at[t], d_ss.at[t], d_rs.at[t]
+
+    for t in range(3):
+        owe(f"d_r{t}", lambda t=t: recv_all(*d_all(t)))
+        owe(f"d_s{t}", lambda t=t: sent_all(*d_all(t)))
+
+    paid("ys_r")
     acc = gp[y].astype(F32)
     for r in range(1, 4):
         acc = acc + yb[lax.rem(y + r, 4)].astype(F32)
@@ -403,12 +498,15 @@
         def _():
             cp.start()
 
-    loop(2, 4, backward)
-
-    dq_all = (dqa[...] * SCALE).astype(BF)
-    for p in range(8):
-        d_s[2, p] = dq_all[:, 128 * p : 128 * p + 128]
-        out_block(2, p)
+    def zs_sent():
+        for kk in range(2):
+            r, cp = zsend(kk)
+
+            @pl.when(r != 0)
+            def _():
+                cp.wait_send()
+
+    owe("zs_s", zs_sent)
 
     def mx():
         return copy_to(ms, mb, m_ss, m_rs, seq_dev(lax.rem(me + 4, 8)))
@@ -418,6 +516,10 @@
 
     def fx_recv(xx):
         return copy_to(fs.at[c], ob.at[xx], f_ss.at[c, xx], f_rs.at[xx], xc_dev(xx, c))
+
+    def zs_recv():
+        for r, step in ((1, 1), (2, 2), (3, -1)):
+            copy_to(zs.at[0], zb.at[r], z_ss.at[0], z_rs.at[r], z_dev(step)).wait_recv()
 
     @pl.when(owner)
     def _():
@@ -426,22 +528,29 @@
         tot = zs[lax.rem(zl, 2)].astype(F32)
         for r in range(1, 4):
             tot = tot + zb[r].astype(F32)
-        ms[...] = tot
+        ms[...] = tot.astype(BF)
         mx().start()
         mx().wait_recv()
         norm = 1.0 / jnp.sqrt(F32(32 * 1024))
-        both = (ms[...] + mb[...]) * norm
-        fs[...] = both.reshape(2, 24, W5)
+        both = (ms[...].astype(F32) + mb[...].astype(F32)) * norm
+        fs[...] = both.reshape(2, 24, W5).astype(BF)
         loop(0, 4, lambda xx: fx(xx, oc).start())
         loop(1, 4, lambda r: fx(lax.rem(x + r, 4), c).start())
         ob[x] = fs[c]
 
-    def d_all(t):
-        return d_s.at[t], d_r.at[t], d_ss.at[t], d_rs.at[t]
-
-    for t, out in ((0, dk_out), (1, dv_out), (2, dq_out)):
-        recv_all(*d_all(t))
+    def own_sent():
+        @pl.when(owner)
+        def _():
+            mx().wait_send()
+            loop(0, 4, lambda xx: fx(xx, oc).wait_send())
+            loop(1, 4, lambda r: fx(lax.rem(x + r, 4), c).wait_send())
+
+    owe("own_s", own_sent)
+
+    for t, out, there in ((0, dk_out, dk_hbm), (1, dv_out, dv_hbm), (2, dq_out, dq_hbm)):
+        paid(f"d_r{t}")
         out[...] = tr(d_r[t].reshape(CH, ROWS)).astype(BF)
+        store(1 + t, out, there)
 
     loop(1, 4, lambda r: fx_recv(lax.rem(x + r, 4)).wait_recv())
 
@@ -450,54 +559,34 @@
         fx_recv(x).wait_recv()
 
     for a in range(TAPS):
-        gw_out[:, a, :] = lanes([ob[b, :, QC * a : QC * a + QC] for b in range(4)])
-
-    for t in range(3):
-        sent_all(*qkv(t))
-        sent_all(*d_all(t))
-    sent_all(att_s, att_r, att_ss, att_rs)
-    sent_all(gs_s, gs_r, gs_ss, gs_rs)
-    loop(1, 4, lambda r: wy(lax.rem(y + r, 4), y).wait_send())
-    loop(1, 4, lambda r: cx(lax.rem(x + r, 4), x).wait_send())
-
-    @pl.when(first)
-    def _():
-        loop(0, 4, lambda p: edge(p, 0).wait_send())
-
-    @pl.when(last)
-    def _():
-        loop(4, 8, lambda p: edge(p, 112).wait_send())
-
-    wz(0, 1, zl).wait_send()
-    wz(1, -1, zl).wait_send()
-    wz(2, far, zl).wait_send()
-    wc(c).wait_send()
-    co.wait_send()
-    loop(1, 4, lambda r: bk(lax.rem(x + r, 4), lax.rem(x + r, 4), x).wait_send())
-    loop(0, 4, lambda xx: hx(xx, oc).wait_send())
-    loop(1, 4, lambda r: hx(lax.rem(x + r, 4), c).wait_send())
-    loop(1, 4, lambda r: ys(r).wait_send())
-    for kk in range(2):
-        r, cp = zsend(kk)
-
-        @pl.when(r != 0)
-        def _():
-            cp.wait_send()
-
-    @pl.when(owner)
-    def _():
-        mx().wait_send()
-        loop(0, 4, lambda xx: fx(xx, oc).wait_send())
-        loop(1, 4, lambda r: fx(lax.rem(x + r, 4), c).wait_send())
+        gw_out[a] = lanes([ob[b, :, QC * a : QC * a + QC].astype(F32) for b in range(4)])
+
+    store(4, gw_out, gw_hbm)
+
+    finish()
+
+
+def hand_over(*refs):
+    ins, outs, held, sem = refs[:5], refs[5:10], refs[10:15], refs[15]
+    reads = [pltpu.make_async_copy(ins[i], held[i], sem.at[0, i]) for i in range(5)]
+    writes = [pltpu.make_async_copy(held[i], outs[i], sem.at[1, i]) for i in range(5)]
+    for read in reads:
+        read.start()
+    for read, write in zip(reads, writes):
+        read.wait()
+        write.start()
+    for write in writes:
+        write.wait()
 
 
 def body(stream_in, queries, key_rows, value_rows, conv_weight, cotangent):
-    x = lax.rem(lax.axis_index("seq"), 4)
-    w = lax.dynamic_slice(conv_weight, (0, 0, x * QC), (24, TAPS, QC)).reshape(24, W5)
     nat = jax.ShapeDtypeStruct((ROWS, CH), BF)
     V = pltpu.VMEM
     blk = (8, HD, ROWS)
-    scratch = [
+    scratch = [V((ROWS, CH), BF) for _ in range(4)] + [
+        V((TAPS, 24, CH), F32),
+    ] + [V((ROWS, CH), BF) for _ in range(5)] + [
+        V((TAPS, 24, CH), BF),
         V((3,) + blk, BF), V((3,) + blk, BF),
         V((1024, HD), BF), V((1024, HD), BF),
         V((1024, 256), F32), V((4, 1024, 256), F32), V((4, 1, 256), F32), V((4, HD, 256), F32),
@@ -508,29 +597,36 @@
         V((4, QC, ROWS), BF), V((2, 4, QC, ROWS), BF), V((2, W5, EXT), BF),
         V(blk, BF), V(blk, BF), V((HD, 1024), F32), V((3,) + blk, BF), V((3,) + blk, BF),
         V((4, 96, W5), BF), V((4, 96, W5), BF), V((2, 48, W5), BF), V((4, 48, W5), BF),
-        V((48, W5), F32), V((48, W5), F32), V((2, 24, W5), F32), V((4, 24, W5), F32),
-        V((8, 128), F32),
+        V((48, W5), BF), V((48, W5), BF), V((2, 24, W5), BF), V((4, 24, W5), BF),
     ]
     D = pltpu.SemaphoreType.DMA
     sems = [
-        D((3, 8)), D((3, 8)), D((8,)), D((8,)), D((8,)), D((8,)), D((3, 8)), D((3, 8)),
+        D((6,)), D((5,)), D((3, 8)), D((3, 8)), D((8,)), D((8,)), D((8,)), D((8,)), D((3, 8)), D((3, 8)),
         D((4,)), D((4,)), D((4,)), D, D, D,
         D((4,)), D((4,)), D((3,)), D((3,)), D, D,
         D((4,)), D((4,)), D((2, 4)), D((2, 4)), D((4,)), D((4,)), D((2,)), D((4,)), D, D,
         D((2, 4)), D((4,)),
     ]
-    vm = pl.BlockSpec(memory_space=pltpu.VMEM)
-    gs, dq, dk, dv, gw = pl.pallas_call(
+    hbm = pl.BlockSpec(memory_space=pl.ANY)
+    shapes = (nat, nat, nat, nat, jax.ShapeDtypeStruct((TAPS, 24, CH), F32))
+    made = pl.pallas_call(
         kernel,
-        out_shape=(nat, nat, nat, nat, jax.ShapeDtypeStruct((24, TAPS, CH), F32)),
-        in_specs=[vm] * 6,
-        out_specs=(vm,) * 5,
+        out_shape=shapes,
+        in_specs=[hbm] * 6,
+        out_specs=(hbm,) * 5,
         scratch_shapes=scratch + sems,
         compiler_params=pltpu.CompilerParams(
-            collective_id=0, has_side_effects=True, vmem_limit_bytes=48 * 1024 * 1024
+            collective_id=0, has_side_effects=True, vmem_limit_bytes=58 * 1024 * 1024
         ),
-    )(stream_in[0], queries[0], key_rows[0], value_rows[0], w, cotangent[0])
-    return gs[None], dq[None], dk[None], dv[None], gw
+    )(stream_in[0], queries[0], key_rows[0], value_rows[0], jnp.transpose(conv_weight, (1, 0, 2)), cotangent[0])
+    gs, dq, dk, dv, gw = pl.pallas_call(
+        hand_over,
+        out_shape=shapes,
+        in_specs=[hbm] * 5,
+        out_specs=(hbm,) * 5,
+        scratch_shapes=[V((ROWS, CH), BF) for _ in range(4)] + [V((TAPS, 24, CH), F32), D((2, 5))],
+    )(*made)
+    return gs[None], dq[None], dk[None], dv[None], jnp.transpose(gw, (1, 0, 2))
 
 
 def solution(mesh):

time: 110 us -> 87.5 us (0.80)
  the two profiles are of different devices: /device:TPU:8 before, /device:TPU:32 now
where the time goes in v2:
time: 87.5 us; the launch traced here: 87.3 us
  Pallas kernels  86.7 us (99%)
    pallas_call x1, Pallas kernels, body(): pl.pallas_call(kernel, out_shape=shapes, in_specs=[hbm] * 6, out_specs=(h...  84.5 us
    pallas_call x1, Pallas kernels, body(): pl.pallas_call(hand_over, out_shape=shapes, in_specs=[hbm] * 5, out_specs...  2.17 us

profile of v2, /device:TPU:32, one launch (start us, length us, event | category | flops | bytes accessed | tf_op | source)
XLA Modules:
  0.0 87.3 jit_solution(9059272987098261119)
XLA Ops:
  0.6 84.5 %shard_map.101 = (bf16[128,768]{1,0:T(8,128)(2,1)}, bf16[128,768]{1,0:T(8,128)(2,1)}, bf16[128,768]{1,0:T(8,128)(2,1)}, bf16[128,768]{1,0:T(8,128)(2,1)}, f32[5,24,768]{2,1,0:T(8,128)}) custom-call(bf16[128,768]{1,0:T(8,128)(2,1)} %bitcast.11, bf16[128,768]{1,0:T(8,128)(2,1)} %bitcast.12, bf16[128,768]{1,0:T(8,128)(2,1)} %bitcast.13, ...), custom_call_target="tpu_custom_call" | custom-call | tf_op jit(solution)/shard_map/pallas_call | solution.py:612
  85.2 2.2 %shard_map.102 = (bf16[128,768]{1,0:T(8,128)(2,1)}, bf16[128,768]{1,0:T(8,128)(2,1)}, bf16[128,768]{1,0:T(8,128)(2,1)}, bf16[128,768]{1,0:T(8,128)(2,1)}, f32[5,24,768]{2,1,0:T(8,128)}) custom-call(bf16[128,768]{1,0:T(8,128)(2,1)} %get-tuple-element.15.refs_0_, bf16[128,768]{1,0:T(8,128)(2,1)} %get-tuple-element.16.refs_1_, ...), custom_call_target="tpu_custom_call" | custom-call | tf_op jit(solution)/shard_map/pallas_call | solution.py:622

commit v3 on v2

--- a/solution.py
+++ b/solution.py
@@ -172,16 +172,28 @@
         wz(1, -1, zl).wait_send()
         wz(2, far, zl).wait_send()
 
+    def start_qkv(t):
+        start_all(*qkv(t))
+        owe(f"qkv_r{t}", lambda: recv_all(*qkv(t)))
+        owe(f"qkv_s{t}", lambda: sent_all(*qkv(t)))
+
+    start_qkv(0)
     wz(0, 1, zl).start()
     wz(1, -1, zl).start()
     wz(2, far, zl).start()
     owe("wz_r", wz_recv_all)
     owe("wz_s", wz_sent_all)
-    for t in range(3):
-        start_all(*qkv(t))
-        owe(f"qkv_r{t}", lambda t=t: recv_all(*qkv(t)))
-        owe(f"qkv_s{t}", lambda t=t: sent_all(*qkv(t)))
-
+    paid("wz_r")
+
+    def wy(yy, slot):
+        return copy_to(wbuf.at[c, slot], wbuf.at[c, slot], wy_ss.at[yy], wy_rs.at[slot], y_dev(yy))
+
+    loop(1, 4, lambda r: wy(lax.rem(y + r, 4), y).start())
+    owe("wy_r", lambda: loop(1, 4, lambda r: wy(lax.rem(y + r, 4), lax.rem(y + r, 4)).wait_recv()))
+    owe("wy_s", lambda: loop(1, 4, lambda r: wy(lax.rem(y + r, 4), y).wait_send()))
+
+    start_qkv(1)
+    start_qkv(2)
     loads[3].wait()
     cblk[x] = tr(c_ref[...]).astype(BF)
     for t in range(3):
@@ -229,15 +241,6 @@
 
     owe("edge_r", edge_recv)
     owe("edge_s", edge_sent)
-    paid("wz_r")
-
-    def wy(yy, slot):
-        return copy_to(wbuf.at[c, slot], wbuf.at[c, slot], wy_ss.at[yy], wy_rs.at[slot], y_dev(yy))
-
-    loop(1, 4, lambda r: wy(lax.rem(y + r, 4), y).start())
-    owe("wy_r", lambda: loop(1, 4, lambda r: wy(lax.rem(y + r, 4), lax.rem(y + r, 4)).wait_recv()))
-    owe("wy_s", lambda: loop(1, 4, lambda r: wy(lax.rem(y + r, 4), y).wait_send()))
-
     paid("qkv_r0")
     for b in range(8):
         kn[128 * b : 128 * b + 128, :] = tr(qkv_r[0, b]).astype(BF)
@@ -470,7 +473,6 @@
     dq_all = (dqa[...] * SCALE).astype(BF)
     for p in range(8):
         d_s[2, p] = dq_all[:, 128 * p : 128 * p + 128]
-        out_block(2, p)
 
     def d_all(t):
         return d_s.at[t], d_r.at[t], d_ss.at[t], d_rs.at[t]
@@ -520,6 +522,12 @@
     def zs_recv():
         for r, step in ((1, 1), (2, 2), (3, -1)):
             copy_to(zs.at[0], zb.at[r], z_ss.at[0], z_rs.at[r], z_dev(step)).wait_recv()
+
+    paid("zs_s")
+
+    @pl.when(jnp.logical_not(owner))
+    def _():
+        loop(0, 8, lambda p: out_block(2, p))
 
     @pl.when(owner)
     def _():
@@ -530,6 +538,7 @@
             tot = tot + zb[r].astype(F32)
         ms[...] = tot.astype(BF)
         mx().start()
+        loop(0, 8, lambda p: out_block(2, p))
         mx().wait_recv()
         norm = 1.0 / jnp.sqrt(F32(32 * 1024))
         both = (ms[...].astype(F32) + mb[...].astype(F32)) * norm

time: 87.5 us -> 86 us (0.983)
  the two profiles are of different devices: /device:TPU:32 before, /device:TPU:176 now
where the time goes in v3:
time: 86 us; the launch traced here: 85.9 us
  Pallas kernels  85.2 us (99%)
    pallas_call x1, Pallas kernels, body(): pl.pallas_call(kernel, out_shape=shapes, in_specs=[hbm] * 6, out_specs=(h...  83.1 us
    pallas_call x1, Pallas kernels, body(): pl.pallas_call(hand_over, out_shape=shapes, in_specs=[hbm] * 5, out_specs...  2.17 us

profile of v3, /device:TPU:176, one launch (start us, length us, event | category | flops | bytes accessed | tf_op | source)
XLA Modules:
  0.0 85.9 jit_solution(6581060498391752319)
XLA Ops:
  0.6 83.1 %shard_map.101 = (bf16[128,768]{1,0:T(8,128)(2,1)}, bf16[128,768]{1,0:T(8,128)(2,1)}, bf16[128,768]{1,0:T(8,128)(2,1)}, bf16[128,768]{1,0:T(8,128)(2,1)}, f32[5,24,768]{2,1,0:T(8,128)}) custom-call(bf16[128,768]{1,0:T(8,128)(2,1)} %bitcast.11, bf16[128,768]{1,0:T(8,128)(2,1)} %bitcast.12, bf16[128,768]{1,0:T(8,128)(2,1)} %bitcast.13, ...), custom_call_target="tpu_custom_call" | custom-call | tf_op jit(solution)/shard_map/pallas_call | solution.py:621
  83.7 2.2 %shard_map.102 = (bf16[128,768]{1,0:T(8,128)(2,1)}, bf16[128,768]{1,0:T(8,128)(2,1)}, bf16[128,768]{1,0:T(8,128)(2,1)}, bf16[128,768]{1,0:T(8,128)(2,1)}, f32[5,24,768]{2,1,0:T(8,128)}) custom-call(bf16[128,768]{1,0:T(8,128)(2,1)} %get-tuple-element.15.refs_0_, bf16[128,768]{1,0:T(8,128)(2,1)} %get-tuple-element.16.refs_1_, ...), custom_call_target="tpu_custom_call" | custom-call | tf_op jit(solution)/shard_map/pallas_call | solution.py:631

commit v4 on v3

--- a/solution.py
+++ b/solution.py
@@ -510,8 +510,8 @@
 
     owe("zs_s", zs_sent)
 
-    def mx():
-        return copy_to(ms, mb, m_ss, m_rs, seq_dev(lax.rem(me + 4, 8)))
+    def mx(cc):
+        return copy_to(ms.at[cc], mb.at[cc], m_ss.at[cc], m_rs.at[cc], seq_dev(lax.rem(me + 4, 8)))
 
     def fx(xx, cc):
         return copy_to(fs.at[cc], ob.at[x], f_ss.at[cc, xx], f_rs.at[x], xc_dev(xx, cc))
@@ -536,21 +536,26 @@
         tot = zs[lax.rem(zl, 2)].astype(F32)
         for r in range(1, 4):
             tot = tot + zb[r].astype(F32)
-        ms[...] = tot.astype(BF)
-        mx().start()
+        ms[...] = tot.reshape(2, 24, W5).astype(BF)
+        mx(0).start()
+        mx(1).start()
         loop(0, 8, lambda p: out_block(2, p))
-        mx().wait_recv()
         norm = 1.0 / jnp.sqrt(F32(32 * 1024))
-        both = (ms[...].astype(F32) + mb[...].astype(F32)) * norm
-        fs[...] = both.reshape(2, 24, W5).astype(BF)
-        loop(0, 4, lambda xx: fx(xx, oc).start())
-        loop(1, 4, lambda r: fx(lax.rem(x + r, 4), c).start())
-        ob[x] = fs[c]
+        for cc in range(2):
+            mx(cc).wait_recv()
+            fs[cc] = ((ms[cc].astype(F32) + mb[cc].astype(F32)) * norm).astype(BF)
+            loop(1, 4, lambda r: fx(lax.rem(x + r, 4), cc).start())
+            pl.when(cc != c)(fx(x, cc).start)
+
+            @pl.when(cc == c)
+            def _():
+                ob[x] = fs[cc]
 
     def own_sent():
         @pl.when(owner)
         def _():
-            mx().wait_send()
+            mx(0).wait_send()
+            mx(1).wait_send()
             loop(0, 4, lambda xx: fx(xx, oc).wait_send())
             loop(1, 4, lambda r: fx(lax.rem(x + r, 4), c).wait_send())
 
@@ -606,14 +611,14 @@
         V((4, QC, ROWS), BF), V((2, 4, QC, ROWS), BF), V((2, W5, EXT), BF),
         V(blk, BF), V(blk, BF), V((HD, 1024), F32), V((3,) + blk, BF), V((3,) + blk, BF),
         V((4, 96, W5), BF), V((4, 96, W5), BF), V((2, 48, W5), BF), V((4, 48, W5), BF),
-        V((48, W5), BF), V((48, W5), BF), V((2, 24, W5), BF), V((4, 24, W5), BF),
+        V((2, 24, W5), BF), V((2, 24, W5), BF), V((2, 24, W5), BF), V((4, 24, W5), BF),
     ]
     D = pltpu.SemaphoreType.DMA
     sems = [
         D((6,)), D((5,)), D((3, 8)), D((3, 8)), D((8,)), D((8,)), D((8,)), D((8,)), D((3, 8)), D((3, 8)),
         D((4,)), D((4,)), D((4,)), D, D, D,
         D((4,)), D((4,)), D((3,)), D((3,)), D, D,
-        D((4,)), D((4,)), D((2, 4)), D((2, 4)), D((4,)), D((4,)), D((2,)), D((4,)), D, D,
+        D((4,)), D((4,)), D((2, 4)), D((2, 4)), D((4,)), D((4,)), D((2,)), D((4,)), D((2,)), D((2,)),
         D((2, 4)), D((4,)),
     ]
     hbm = pl.BlockSpec(memory_space=pl.ANY)

time: 86 us -> 85.4 us (level); the launches traced: 85.9 us -> 84.3 us
  Pallas kernels: 85.2 us -> 83.7 us
    pallas_call x1, Pallas kernels: 83.1 us -> 81.5 us  [body(): pl.pallas_call(kernel, out_shape=shapes, in_specs=[hbm] * 6, out_specs=(h...]
where the time goes in v4:
time: 85.4 us; the launch traced here: 84.3 us
  Pallas kernels  83.7 us (98%)
    pallas_call x1, Pallas kernels, body(): pl.pallas_call(kernel, out_shape=shapes, in_specs=[hbm] * 6, out_specs=(h...  81.5 us
    pallas_call x1, Pallas kernels, body(): pl.pallas_call(hand_over, out_shape=shapes, in_specs=[hbm] * 5, out_specs...  2.17 us

profile of v4, /device:TPU:176, one launch (start us, length us, event | category | flops | bytes accessed | tf_op | source)
XLA Modules:
  0.0 84.3 jit_solution(3471794579668092547)
XLA Ops:
  0.6 81.5 %shard_map.101 = (bf16[128,768]{1,0:T(8,128)(2,1)}, bf16[128,768]{1,0:T(8,128)(2,1)}, bf16[128,768]{1,0:T(8,128)(2,1)}, bf16[128,768]{1,0:T(8,128)(2,1)}, f32[5,24,768]{2,1,0:T(8,128)}) custom-call(bf16[128,768]{1,0:T(8,128)(2,1)} %bitcast.11, bf16[128,768]{1,0:T(8,128)(2,1)} %bitcast.12, bf16[128,768]{1,0:T(8,128)(2,1)} %bitcast.13, ...), custom_call_target="tpu_custom_call" | custom-call | tf_op jit(solution)/shard_map/pallas_call | solution.py:626
  82.1 2.2 %shard_map.102 = (bf16[128,768]{1,0:T(8,128)(2,1)}, bf16[128,768]{1,0:T(8,128)(2,1)}, bf16[128,768]{1,0:T(8,128)(2,1)}, bf16[128,768]{1,0:T(8,128)(2,1)}, f32[5,24,768]{2,1,0:T(8,128)}) custom-call(bf16[128,768]{1,0:T(8,128)(2,1)} %get-tuple-element.15.refs_0_, bf16[128,768]{1,0:T(8,128)(2,1)} %get-tuple-element.16.refs_1_, ...), custom_call_target="tpu_custom_call" | custom-call | tf_op jit(solution)/shard_map/pallas_call | solution.py:636
